TPU v7x, 32 devices: a whole 2x2x4 slice. The times are simulated.
32 devices in a mesh: dp: 8 (over z, core), tp: 4 (over y, x).
Axes of the slice: x: 2, y: 2, z: 4, core: 2. Of those that a mesh axis runs over, the one named last changes fastest.
Arguments:
- student_hidden: bfloat16 [1152, 3456], P('dp'), may hold values from -6 to 6
- norm_gain: float32 [3456], replicated, may hold values from 0.25 to 1.75
- projection: bfloat16 [3456, 8192], P(None, 'tp'), may hold values from -0.109375 to 0.109375
- teacher_partials: bfloat16 [4, 1152, 8192], P('tp', 'dp'), may hold values from -5 to 5
- teacher_residual: bfloat16 [1152, 8192], P('dp', 'tp'), may hold values from -90 to 90
- owner: int32 [1152], P('dp'), may hold values from 0 to 1151, as said below
Outputs:
- grad_scaled: float32 [3456, 8192], P('dp', 'tp')
Inputs may be any that keep to these rules, and one draw needn't show every extreme that they name: owner is a permutation of all token indices; the 144 teacher rows of each index of dp hold exactly 18 tokens owned by each index of dp.
All inputs are finite; a program needn't handle non-finite values.
Results may differ from a plain program's by a relative error of at most 0.009.
Values may be sent and summed in bfloat16 or wider, within the bound.
A program may use at most 128 MiB of HBM per device.

v0:
```python
import jax
import jax.numpy as jnp
from jax import lax
from jax.sharding import PartitionSpec as P


def agree(largest):
    return lax.pmax(largest, ("dp", "tp")) + 1e-06


def rounded_terms(partial_value, scale):
    return lax.optimization_barrier((partial_value / scale).astype(jnp.bfloat16)).astype(
        jnp.float32
    )


def per_device(student_hidden, norm_gain, projection, teacher_partials, teacher_residual, owner):
    columns = projection.shape[1]
    rows_dev = student_hidden.shape[0]
    terms_in = teacher_partials[0].astype(jnp.float32)
    summed_all = lax.psum(terms_in.astype(jnp.bfloat16), "tp").astype(jnp.float32)
    summed = lax.dynamic_slice_in_dim(summed_all, lax.axis_index("tp") * columns, columns, 1)
    teacher = (teacher_residual.astype(jnp.float32) + summed).astype(jnp.bfloat16)
    groups = lax.axis_size("dp")
    slots = rows_dev // groups
    destination = owner // rows_dev
    order = jnp.argsort(destination, stable=True)
    outgoing = teacher[order].reshape(groups, slots, columns)
    outgoing_owner = owner[order].reshape(groups, slots)
    arrived, arrived_owner = (
        lax.all_to_all(outgoing, "dp", split_axis=0, concat_axis=0, tiled=True),
        lax.all_to_all(outgoing_owner, "dp", split_axis=0, concat_axis=0, tiled=True),
    )
    placing = jnp.argsort(arrived_owner.reshape(-1) % rows_dev)
    target = arrived.reshape(rows_dev, columns)[placing]
    values = student_hidden.astype(jnp.float32)
    inverse = lax.rsqrt(jnp.mean(values * values, axis=-1, keepdims=True) + 1e-05)
    normed = (values * inverse * norm_gain).astype(jnp.bfloat16)
    pred = jnp.dot(normed, projection, preferred_element_type=jnp.float32)
    diff = (pred - target.astype(jnp.float32)).astype(jnp.bfloat16)
    feature_share = normed.shape[1] // groups
    blocks = lax.all_to_all(normed, "dp", split_axis=1, concat_axis=0, tiled=True).reshape(
        groups, rows_dev, feature_share
    )
    errors = lax.all_gather(diff, "dp", axis=0, tiled=True).reshape(groups, rows_dev, columns)
    partials = jnp.einsum("dsr,dsc->drc", blocks, errors, preferred_element_type=jnp.float32)
    scale = agree(jnp.max(jnp.abs(partials)))
    grad_scaled = jnp.sum(rounded_terms(partials, scale), axis=0)
    return grad_scaled


def solution(mesh):
    placed = (P("dp", None), P(), P(None, "tp"), P("tp", "dp", None), P("dp", "tp"), P("dp"))
    return jax.shard_map(
        per_device, mesh=mesh, in_specs=placed, out_specs=P("dp", "tp"), check_vma=False
    )
```

profile of v0, /device:TPU:12, one launch (start us, length us, event | category | flops | bytes accessed | tf_op | source)
XLA Modules:
  0.0 277.4 jit_solution(12854644300265450455)
XLA Ops:
  6.5 0.0 copy-start
  6.5 0.0 copy-start.1
  6.5 0.0 copy-start.2
  6.5 0.0 all-reduce.2.cloned.1.call-start
  6.5 0.7 all-reduce.2.cloned.1.call-update
  7.3 0.0 copy-done
  7.3 3.2 %sort.34 = (s32[144]{0:T(256)}, s32[144]{0:T(256)S(1)}) sort(s32[144]{0:T(256)S(1)} %and_select_fusion.1, s32[144]{0:T(256)S(1)} %iota.8), dimensions={0}, to_apply=%region_2.3 | sort | flops 1152 | bytes 2304 | tf_op jit(solution)/shard_map/jit(argsort)/sort | solution.py:27
  10.5 1.6 gather_fusion.1
  12.1 0.7 all_to_all.25
  12.8 5.3 %all-to-all-start.2 = ((s32[8,1,18]{2,1,0:T(1,128)}), s32[8,1,18]{2,1,0:T(1,128)S(1)}, u32[]{:S(2)}, u32[]{:S(2)}) async-start(s32[8,1,18]{2,1,0:T(1,128)} %all_to_all.25), calls=%async_computation.2 | async-start | bytes 8192 | tf_op jit(solution)/shard_map/all_to_all | solution.py:32
  18.1 0.0 copy-done.1
  18.1 0.3 fusion.1
  18.4 66.9 %all-reduce.2.cloned.1.call-done = bf16[144,8192]{1,0:T(8,128)(2,1)} async-done(((bf16[144,8192]{1,0:T(8,128)(2,1)}), bf16[144,8192]{1,0:T(8,128)(2,1)}) %all-reduce.2.cloned.1.call-update) | async-done | bytes 2359312 | tf_op jit(solution)/shard_map/psum | solution.py:21
  85.3 0.0 copy-done.2
  85.3 1.3 add_convert_fusion
  86.6 1.0 gather_fusion
  87.6 0.0 copy-start.3
  87.6 1.1 reshape.31
  88.7 0.0 all-to-all-done.2
  88.7 5.1 %all-to-all-start.1 = ((bf16[8,18,2048]{2,1,0:T(8,128)(2,1)}), bf16[8,18,2048]{2,1,0:T(8,128)(2,1)S(1)}, u32[]{:S(2)}, u32[]{:S(2)}) async-start(bf16[8,18,2048]{2,1,0:T(8,128)(2,1)} %reshape.31), calls=%async_computation.1 | async-start | bytes 1572864 | tf_op jit(solution)/shard_map/all_to_all | solution.py:31
  93.8 0.0 all-gather.2.cloned.1.call-start
  93.8 0.0 copy-done.3
  93.8 0.3 fusion.3
  94.1 0.1 rem.23
  94.2 3.2 %sort.35 = (s32[144]{0:T(256)}, s32[144]{0:T(256)S(1)}) sort(s32[144]{0:T(256)S(1)} %and_select_fusion, s32[144]{0:T(256)S(1)} %iota.9), dimensions={0}, to_apply=%region_3.4 | sort | flops 1152 | bytes 2304 | tf_op jit(solution)/shard_map/jit(argsort)/sort | solution.py:34
  97.5 13.8 %all-to-all-done.1 = bf16[8,18,2048]{2,1,0:T(8,128)(2,1)S(1)} async-done(((bf16[8,18,2048]{2,1,0:T(8,128)(2,1)}), bf16[8,18,2048]{2,1,0:T(8,128)(2,1)S(1)}, u32[]{:S(2)}, u32[]{:S(2)}) %all-to-all-start.1) | async-done | bytes 589856 | tf_op jit(solution)/shard_map/all_to_all | solution.py:31
  111.3 0.2 reshape.32
  111.5 1.0 gather_fusion.2
  112.5 8.4 %fusion = bf16[144,2048]{1,0:T(8,128)(2,1)} fusion(bf16[144,3456]{1,0:T(8,128)(2,1)S(1)} %fusion.3, bf16[3456,2048]{1,0:T(8,128)(2,1)} %param.8, bf16[144,2048]{1,0:T(8,128)(2,1)S(1)} %gather_fusion.2), kind=kOutput, calls=%fused_computation.9 | convolution fusion | flops 2039316480 | bytes 16330752 | tf_op jit(solution)/shard_map/dot_general | solution.py:39
  120.9 0.0 all-gather.2.cloned.1.call-update
  120.9 2.7 all_to_all.21
  123.6 0.4 copy.7
  123.9 62.7 %all_to_all.30 = bf16[144,8,432]{2,0,1:T(8,128)(2,1)S(1)} all-to-all(bf16[144,8,432]{2,0,1:T(8,128)(2,1)S(1)} %copy.7), channel_id=1, replica_groups=mesh['dp'=8,'tp'=4] {'dp'}, dimensions={1} | all-to-all | bytes 1990656 | tf_op jit(solution)/shard_map/all_to_all | solution.py:42
  186.7 8.5 %all-gather.2.cloned.1.call-done = bf16[1152,2048]{1,0:T(8,128)(2,1)} async-done(((bf16[144,2048]{1,0:T(8,128)(2,1)}), bf16[1152,2048]{1,0:T(8,128)(2,1)}) %all-gather.2.cloned.1.call-update) | async-done | bytes 4718608 | tf_op jit(solution)/shard_map/all_gather | solution.py:45
  195.1 16.4 %abs_reduce_fusion = (f32[]{:T(128)}, f32[8,432,2048]{2,1,0:T(8,128)}) fusion(bf16[8,144,2048]{2,1,0:T(8,128)(2,1)} %bitcast.10, bf16[144,8,432]{2,0,1:T(8,128)(2,1)S(1)} %all_to_all.30), kind=kOutput, calls=%fused_computation.5 | convolution fusion | flops 2052587520 | bytes 34025476 | tf_op jit(solution)/shard_map/dsr,dsc->drc/dot_general | solution.py:46
  211.5 42.5 %pmax.7 = f32[]{:T(128)} all-reduce(f32[]{:T(128)} %get-tuple-element.9), channel_id=1, replica_groups=mesh['dp'=8,'tp'=4] {'dp','tp'}, use_global_device_ids=true, to_apply=%region_5.6 | all-reduce | flops 1 | bytes 8 | tf_op jit(solution)/shard_map/pmax | solution.py:8
  254.7 11.1 %divide_convert_fusion = bf16[8,432,2048]{2,1,0:T(8,128)(2,1)S(1)} fusion(f32[8,432,2048]{2,1,0:T(8,128)} %get-tuple-element.10, f32[]{:T(128)S(6)} %add.43), kind=kLoop, calls=%fused_computation.4 | loop fusion | flops 14155776 | bytes 42467332 | tf_op jit(solution)/shard_map/convert_element_type | solution.py:12
  265.8 4.8 %convert_reduce_fusion = f32[432,2048]{1,0:T(8,128)} fusion(bf16[8,432,2048]{2,1,0:T(8,128)(2,1)S(1)} %divide_convert_fusion), kind=kLoop, calls=%fused_computation.3 | loop fusion | flops 13271040 | bytes 17694720 | tf_op jit(solution)/shard_map/reduce_sum | solution.py:48
  (10 shorter events, 0.1 us)
Async XLA Ops:
  6.5 0.7 copy-start
  6.5 11.6 %copy-start.1 = (bf16[144,3456]{1,0:T(8,128)(2,1)S(1)}, bf16[144,3456]{1,0:T(8,128)(2,1)}, u32[]{:S(2)}) copy-start(bf16[144,3456]{1,0:T(8,128)(2,1)} %param.6) | copy-start | bytes 2985988
  6.5 78.8 %copy-start.2 = (bf16[144,2048]{1,0:T(8,128)(2,1)S(1)}, bf16[144,2048]{1,0:T(8,128)(2,1)}, u32[]{:S(2)}) copy-start(bf16[144,2048]{1,0:T(8,128)(2,1)} %param.10) | copy-start | bytes 1769476
  6.5 78.8 %all-reduce.2.cloned.1.call-start = ((), (), s32[]{:S(2)}) async-start(), calls=%async_computation.3 | async-start | bytes 4718592 | tf_op jit(solution)/shard_map/psum | solution.py:21
  12.8 75.9 %all-to-all-start.2 = ((s32[8,1,18]{2,1,0:T(1,128)}), s32[8,1,18]{2,1,0:T(1,128)S(1)}, u32[]{:S(2)}, u32[]{:S(2)}) async-start(s32[8,1,18]{2,1,0:T(1,128)} %all_to_all.25), calls=%async_computation.2 | async-start | bytes 8192 | tf_op jit(solution)/shard_map/all_to_all | solution.py:32
  87.6 6.2 %copy-start.3 = (f32[3456]{0:T(1024)S(1)}, f32[3456]{0:T(1024)}, u32[]{:S(2)}) copy-start(f32[3456]{0:T(1024)} %param.7) | copy-start | bytes 41476
  88.7 22.6 %all-to-all-start.1 = ((bf16[8,18,2048]{2,1,0:T(8,128)(2,1)}), bf16[8,18,2048]{2,1,0:T(8,128)(2,1)S(1)}, u32[]{:S(2)}, u32[]{:S(2)}) async-start(bf16[8,18,2048]{2,1,0:T(8,128)(2,1)} %reshape.31), calls=%async_computation.1 | async-start | bytes 1572864 | tf_op jit(solution)/shard_map/all_to_all | solution.py:31
  93.8 101.3 %all-gather.2.cloned.1.call-start = ((), (), s32[]{:S(2)}) async-start(), calls=%async_computation.4 | async-start | bytes 5308416 | tf_op jit(solution)/shard_map/all_gather | solution.py:45
Sparse Core Ops, SparseCore 0:
  10.5 74.8 all-reduce.1
  121.0 74.0 all-gather.1
where the time goes:
time: 278 us; the launch traced here: 277 us
  blocking collectives  105 us (38%)
  waiting for transfers between devices  90 us (32%)
  matrix products  24.7 us (9%)
  other arithmetic  24.2 us (9%)
  between operations  14.1 us (5%)
  starting transfers between devices  10.5 us (4%)
  local copies, waits for them, and re-layouts  8.65 us (3%)
    psum x1, waiting for transfers between devices, per_device(): lax.psum(terms_in.astype(jnp.bfloat16), 'tp').astype(jnp.float32)  66.9 us
    all_to_all x1, blocking collectives, per_device(): lax.all_to_all(normed, 'dp', split_axis=1, concat_axis=0, tiled=True)  62.7 us
    pmax x1, blocking collectives, agree(): return lax.pmax(largest, ('dp', 'tp')) + 1e-06  42.5 us
    dot_general x1, matrix products, per_device(): jnp.einsum('dsr,dsc->drc', blocks, errors, preferred_element_type=jnp.flo...  16.4 us
    all_to_all x1, waiting for transfers between devices, per_device(): lax.all_to_all(outgoing, 'dp', split_axis=0, concat_axis=0, tiled=True)  13.8 us
    convert_element_type x1, other arithmetic, rounded_terms(): (partial_value / scale).astype(jnp.bfloat16)  11.1 us
    all_gather x1, waiting for transfers between devices, per_device(): lax.all_gather(diff, 'dp', axis=0, tiled=True)  8.48 us
    dot_general x1, matrix products, per_device(): pred = jnp.dot(normed, projection, preferred_element_type=jnp.float32)  8.37 us
  transfers between devices with their start and end apart: 4, of which 3 were waited for; matrix products, arithmetic and copies ran while one was open for 4% of the time, Pallas kernels for 0%

commit v1 on v0

--- a/solution.py
+++ b/solution.py
@@ -18,7 +18,9 @@
     columns = projection.shape[1]
     rows_dev = student_hidden.shape[0]
     terms_in = teacher_partials[0].astype(jnp.float32)
-    summed_all = lax.psum(terms_in.astype(jnp.bfloat16), "tp").astype(jnp.float32)
+    summed_all = jnp.sum(lax.all_gather(terms_in.astype(jnp.bfloat16), "tp"), axis=0).astype(
+        jnp.float32
+    )
     summed = lax.dynamic_slice_in_dim(summed_all, lax.axis_index("tp") * columns, columns, 1)
     teacher = (teacher_residual.astype(jnp.float32) + summed).astype(jnp.bfloat16)
     groups = lax.axis_size("dp")

time: 278 us -> 306 us (1.10)
  waiting for transfers between devices: 90 us -> 111 us
  other arithmetic: 24.2 us -> 31.6 us
    all_gather x0 -> x1, waiting for transfers between devices: none -> 88.1 us  [per_device(): lax.all_gather(terms_in.astype(jnp.bfloat16), 'tp')]
    psum x1 -> x0, waiting for transfers between devices: 66.9 us -> none  [per_device(): lax.psum(terms_in.astype(jnp.bfloat16), 'tp').astype(jnp.float32)]
    reduce_sum x0 -> x1, other arithmetic: none -> 7.52 us  [per_device(): jnp.sum(lax.all_gather(terms_in.astype(jnp.bfloat16), 'tp'), axis=0)]
  transfers between devices with their start and end apart: 4 -> 4, of which waited for: 3 -> 3; matrix products, arithmetic and copies ran while one was open for 4% -> 6% of each run, Pallas kernels for 0% -> 0%
where the time goes in v1:
time: 306 us
  waiting for transfers between devices  111 us (36%)
  blocking collectives  105 us (34%)
  other arithmetic  31.6 us (10%)
  matrix products  24.7 us (8%)
  between operations  14.2 us (5%)
  starting transfers between devices  10.5 us (3%)
  local copies, waits for them, and re-layouts  8.64 us (3%)
    all_gather x1, waiting for transfers between devices, per_device(): lax.all_gather(terms_in.astype(jnp.bfloat16), 'tp')  88.1 us
    all_to_all x1, blocking collectives, per_device(): lax.all_to_all(normed, 'dp', split_axis=1, concat_axis=0, tiled=True)  62.7 us
    pmax x1, blocking collectives, agree(): return lax.pmax(largest, ('dp', 'tp')) + 1e-06  42.4 us
    dot_general x1, matrix products, per_device(): jnp.einsum('dsr,dsc->drc', blocks, errors, preferred_element_type=jnp.flo...  16.3 us
    all_to_all x1, waiting for transfers between devices, per_device(): lax.all_to_all(outgoing, 'dp', split_axis=0, concat_axis=0, tiled=True)  13.8 us
    convert_element_type x1, other arithmetic, rounded_terms(): (partial_value / scale).astype(jnp.bfloat16)  11.1 us
    all_gather x1, waiting for transfers between devices, per_device(): lax.all_gather(diff, 'dp', axis=0, tiled=True)  8.44 us
    dot_general x1, matrix products, per_device(): pred = jnp.dot(normed, projection, preferred_element_type=jnp.float32)  8.42 us
  transfers between devices with their start and end apart: 4, of which 3 were waited for; matrix products, arithmetic and copies ran while one was open for 6% of the time, Pallas kernels for 0%

profile of v1, /device:TPU:12, one launch (start us, length us, event | category | flops | bytes accessed | tf_op | source)
XLA Modules:
  0.0 305.8 jit_solution(1552817123931303720)
XLA Ops:
  6.5 0.0 copy-start
  6.5 0.0 copy-start.1
  6.5 0.0 all-gather.3.cloned.1.call-start
  6.5 0.7 all-gather.3.cloned.1.call-update
  7.3 0.0 copy-done
  7.3 3.2 %sort.34 = (s32[144]{0:T(256)}, s32[144]{0:T(256)S(1)}) sort(s32[144]{0:T(256)S(1)} %and_select_fusion.1, s32[144]{0:T(256)S(1)} %iota.8), dimensions={0}, to_apply=%region_2.3 | sort | flops 1152 | bytes 2304 | tf_op jit(solution)/shard_map/jit(argsort)/sort | solution.py:29
  10.5 1.6 gather_fusion.1
  12.1 0.7 all_to_all.25
  12.8 5.3 %all-to-all-start.2 = ((s32[8,1,18]{2,1,0:T(1,128)}), s32[8,1,18]{2,1,0:T(1,128)S(1)}, u32[]{:S(2)}, u32[]{:S(2)}) async-start(s32[8,1,18]{2,1,0:T(1,128)} %all_to_all.25), calls=%async_computation.2 | async-start | bytes 8192 | tf_op jit(solution)/shard_map/all_to_all | solution.py:34
  18.1 0.0 copy-done.1
  18.1 0.3 fusion.1
  18.4 0.0 copy-start.2
  18.4 88.1 %all-gather.3.cloned.1.call-done = bf16[4,144,8192]{2,1,0:T(8,128)(2,1)} async-done(((bf16[1,144,8192]{2,1,0:T(8,128)(2,1)}), bf16[4,144,8192]{2,1,0:T(8,128)(2,1)}) %all-gather.3.cloned.1.call-update) | async-done | bytes 9437200 | tf_op jit(solution)/shard_map/all_gather | solution.py:21
  106.5 7.5 %reduce_sum.31 = bf16[144,8192]{1,0:T(8,128)(2,1)} reduce(bf16[4,144,8192]{2,1,0:T(8,128)(2,1)} %all-gather.3.cloned.1.call-done, bf16[]{:T(256)} %constant.18.clone.1), dimensions={0}, to_apply=%region_1.2 | reduce | flops 3538944 | bytes 11796482 | tf_op jit(solution)/shard_map/reduce_sum | solution.py:21
  114.0 0.0 copy-done.2
  114.0 1.2 add_convert_fusion
  115.3 1.0 gather_fusion
  116.2 0.0 copy-start.3
  116.3 1.1 reshape.32
  117.3 0.0 all-to-all-done.2
  117.3 5.1 %all-to-all-start.1 = ((bf16[8,18,2048]{2,1,0:T(8,128)(2,1)}), bf16[8,18,2048]{2,1,0:T(8,128)(2,1)S(1)}, u32[]{:S(2)}, u32[]{:S(2)}) async-start(bf16[8,18,2048]{2,1,0:T(8,128)(2,1)} %reshape.32), calls=%async_computation.1 | async-start | bytes 1572864 | tf_op jit(solution)/shard_map/all_to_all | solution.py:33
  122.5 0.0 all-gather.5.cloned.1.call-start
  122.5 0.0 copy-done.3
  122.5 0.3 fusion.3
  122.8 0.1 rem.23
  122.9 3.2 %sort.35 = (s32[144]{0:T(256)}, s32[144]{0:T(256)S(1)}) sort(s32[144]{0:T(256)S(1)} %and_select_fusion, s32[144]{0:T(256)S(1)} %iota.9), dimensions={0}, to_apply=%region_3.4 | sort | flops 1152 | bytes 2304 | tf_op jit(solution)/shard_map/jit(argsort)/sort | solution.py:36
  126.1 13.8 %all-to-all-done.1 = bf16[8,18,2048]{2,1,0:T(8,128)(2,1)S(1)} async-done(((bf16[8,18,2048]{2,1,0:T(8,128)(2,1)}), bf16[8,18,2048]{2,1,0:T(8,128)(2,1)S(1)}, u32[]{:S(2)}, u32[]{:S(2)}) %all-to-all-start.1) | async-done | bytes 589856 | tf_op jit(solution)/shard_map/all_to_all | solution.py:33
  140.0 0.2 reshape.33
  140.1 1.0 gather_fusion.2
  141.1 8.4 %fusion = bf16[144,2048]{1,0:T(8,128)(2,1)} fusion(bf16[144,3456]{1,0:T(8,128)(2,1)S(1)} %fusion.3, bf16[3456,2048]{1,0:T(8,128)(2,1)} %param.8, bf16[144,2048]{1,0:T(8,128)(2,1)S(1)} %gather_fusion.2), kind=kOutput, calls=%fused_computation.9 | convolution fusion | flops 2039316480 | bytes 16330752 | tf_op jit(solution)/shard_map/dot_general | solution.py:41
  149.6 0.0 all-gather.5.cloned.1.call-update
  149.6 2.7 all_to_all.21
  152.3 0.4 copy.8
  152.6 62.7 %all_to_all.30 = bf16[144,8,432]{2,0,1:T(8,128)(2,1)S(1)} all-to-all(bf16[144,8,432]{2,0,1:T(8,128)(2,1)S(1)} %copy.8), channel_id=1, replica_groups=mesh['dp'=8,'tp'=4] {'dp'}, dimensions={1} | all-to-all | bytes 1990656 | tf_op jit(solution)/shard_map/all_to_all | solution.py:44
  215.3 8.4 %all-gather.5.cloned.1.call-done = bf16[1152,2048]{1,0:T(8,128)(2,1)} async-done(((bf16[144,2048]{1,0:T(8,128)(2,1)}), bf16[1152,2048]{1,0:T(8,128)(2,1)}) %all-gather.5.cloned.1.call-update) | async-done | bytes 4718608 | tf_op jit(solution)/shard_map/all_gather | solution.py:47
  223.8 16.3 %abs_reduce_fusion = (f32[]{:T(128)}, f32[8,432,2048]{2,1,0:T(8,128)}) fusion(bf16[8,144,2048]{2,1,0:T(8,128)(2,1)} %bitcast.9, bf16[144,8,432]{2,0,1:T(8,128)(2,1)S(1)} %all_to_all.30), kind=kOutput, calls=%fused_computation.5 | convolution fusion | flops 2052587520 | bytes 34025476 | tf_op jit(solution)/shard_map/dsr,dsc->drc/dot_general | solution.py:48
  240.1 42.4 %pmax.7 = f32[]{:T(128)} all-reduce(f32[]{:T(128)} %get-tuple-element.9), channel_id=1, replica_groups=mesh['dp'=8,'tp'=4] {'dp','tp'}, use_global_device_ids=true, to_apply=%region_5.6 | all-reduce | flops 1 | bytes 8 | tf_op jit(solution)/shard_map/pmax | solution.py:8
  283.2 11.1 %divide_convert_fusion = bf16[8,432,2048]{2,1,0:T(8,128)(2,1)S(1)} fusion(f32[8,432,2048]{2,1,0:T(8,128)} %get-tuple-element.10, f32[]{:T(128)S(6)} %add.41), kind=kLoop, calls=%fused_computation.4 | loop fusion | flops 14155776 | bytes 42467332 | tf_op jit(solution)/shard_map/convert_element_type | solution.py:12
  294.3 4.7 %convert_reduce_fusion = f32[432,2048]{1,0:T(8,128)} fusion(bf16[8,432,2048]{2,1,0:T(8,128)(2,1)S(1)} %divide_convert_fusion), kind=kLoop, calls=%fused_computation.3 | loop fusion | flops 13271040 | bytes 17694720 | tf_op jit(solution)/shard_map/reduce_sum | solution.py:50
  (10 shorter events, 0.1 us)
Async XLA Ops:
  6.5 0.7 copy-start
  6.5 11.6 %copy-start.1 = (bf16[144,3456]{1,0:T(8,128)(2,1)S(1)}, bf16[144,3456]{1,0:T(8,128)(2,1)}, u32[]{:S(2)}) copy-start(bf16[144,3456]{1,0:T(8,128)(2,1)} %param.6) | copy-start | bytes 2985988
  6.5 100.0 %all-gather.3.cloned.1.call-start = ((), (), s32[]{:S(2)}) async-start(), calls=%async_computation.3 | async-start | bytes 11796480 | tf_op jit(solution)/shard_map/all_gather | solution.py:21
  12.8 104.5 %all-to-all-start.2 = ((s32[8,1,18]{2,1,0:T(1,128)}), s32[8,1,18]{2,1,0:T(1,128)S(1)}, u32[]{:S(2)}, u32[]{:S(2)}) async-start(s32[8,1,18]{2,1,0:T(1,128)} %all_to_all.25), calls=%async_computation.2 | async-start | bytes 8192 | tf_op jit(solution)/shard_map/all_to_all | solution.py:34
  18.4 95.6 %copy-start.2 = (bf16[144,2048]{1,0:T(8,128)(2,1)S(1)}, bf16[144,2048]{1,0:T(8,128)(2,1)}, u32[]{:S(2)}) copy-start(bf16[144,2048]{1,0:T(8,128)(2,1)} %param.10) | copy-start | bytes 1769476
  116.2 6.2 %copy-start.3 = (f32[3456]{0:T(1024)S(1)}, f32[3456]{0:T(1024)}, u32[]{:S(2)}) copy-start(f32[3456]{0:T(1024)} %param.7) | copy-start | bytes 41476
  117.3 22.6 %all-to-all-start.1 = ((bf16[8,18,2048]{2,1,0:T(8,128)(2,1)}), bf16[8,18,2048]{2,1,0:T(8,128)(2,1)S(1)}, u32[]{:S(2)}, u32[]{:S(2)}) async-start(bf16[8,18,2048]{2,1,0:T(8,128)(2,1)} %reshape.32), calls=%async_computation.1 | async-start | bytes 1572864 | tf_op jit(solution)/shard_map/all_to_all | solution.py:33
  122.5 101.3 %all-gather.5.cloned.1.call-start = ((), (), s32[]{:S(2)}) async-start(), calls=%async_computation.4 | async-start | bytes 5308416 | tf_op jit(solution)/shard_map/all_gather | solution.py:47
Sparse Core Ops, SparseCore 0:
  9.2 97.2 all-gather.2
  149.7 74.0 all-gather.4
